TPU v7x, 128 devices: a whole 4x4x4 slice. The times are simulated.
128 devices in a mesh: lon: 16 (over y, z_hi, core), lat: 8 (over z_lo, x).
Axes of the slice: x: 4, y: 4, z: 4 (z_hi: 2, z_lo: 2; z = z_hi * 2 + z_lo), core: 2. Of those that a mesh axis runs over, the one named last changes fastest.
Arguments:
- members: bfloat16 [3, 256, 2880, 128], P(None, 'lat', 'lon'), may hold values from -6 to 6
- background: bfloat16 [3, 256, 2880], P(None, 'lat', 'lon'), may hold values from -6 to 6
Outputs:
- modes: float32 [3, 256, 2880, 128], P(None, 'lat', 'lon')
- r_factor: float32 [128, 128], replicated
All inputs are finite; a program needn't handle non-finite values.
Results may differ from a plain program's by a relative error of at most 0.0076.
The roundings to bfloat16 on the way count: a program that leaves them out, or rounds other values in their place, can miss the bound.
Values may be sent and summed in bfloat16 or wider, within the bound.
A program may use at most 64 MiB of HBM per device.

v0:
```python
import math
import jax
import jax.numpy as jnp
from jax import lax
from jax.sharding import PartitionSpec as P


def extended(shard, sides, width, wrap):
    for axis, dim in sides:
        peers, length = (lax.axis_size(axis), shard.shape[dim])
        up = [(i, (i + 1) % peers) for i in range(peers if wrap else peers - 1)]
        down = [(j, i) for i, j in up]
        last = lax.slice_in_dim(shard, length - width, length, axis=dim)
        leading = lax.slice_in_dim(shard, 0, width, axis=dim)
        before = lax.ppermute(last, axis, up)
        after = lax.ppermute(leading, axis, down)
        shard = jnp.concatenate([before, shard, after], axis=dim)
    return shard


def row_coefs(glob, nlat):
    phi = (0.125 * (glob.astype(jnp.float32) + 0.5) - 0.0625 * nlat) * (math.pi / 180.0)
    kx = 0.05 + 0.2 * (1.0 - jnp.cos(phi))
    weight = jnp.sqrt(jnp.cos(phi))
    return (kx, weight)


def smooth_pass(padded, kx):
    centre = padded[:, 1:-1, 1:-1]
    east_west = padded[:, 1:-1, 2:] + padded[:, 1:-1, :-2] - 2.0 * centre
    north_south = padded[:, 2:, 1:-1] + padded[:, :-2, 1:-1] - 2.0 * centre
    return centre + kx[None, :, None, None] * east_west + 0.2 * north_south


def chol_upper(gram):
    order = gram.shape[0]
    index = jnp.arange(order)

    def column(j, lower):
        row_j = lax.dynamic_slice_in_dim(lower, j, 1, 0)[0]
        col_g = lax.dynamic_slice_in_dim(gram, j, 1, 1)[:, 0]
        resid = col_g - jnp.dot(lower, row_j, precision=lax.Precision.HIGHEST)
        pivot = jnp.sqrt(jnp.sum(jnp.where(index == j, resid, 0.0)))
        col_new = jnp.where(index >= j, resid / pivot, 0.0)
        return lower + col_new[:, None] * (index[None, :] == j).astype(jnp.float32)

    lower = lax.fori_loop(0, order, column, jnp.zeros((order, order), jnp.float32))
    return lower.T


def upper_inverse(upper):
    order = upper.shape[0]
    index = jnp.arange(order)
    ident = jnp.eye(order, dtype=jnp.float32)

    def row_step(step, solved):
        i = order - 1 - step
        row_u = lax.dynamic_slice_in_dim(upper, i, 1, 0)[0]
        diag = jnp.sum(jnp.where(index == i, row_u, 0.0))
        above = jnp.where(index > i, row_u, 0.0)
        unit = lax.dynamic_slice_in_dim(ident, i, 1, 0)[0]
        new_row = (unit - jnp.dot(above, solved, precision=lax.Precision.HIGHEST)) / diag
        return solved + (index == i).astype(jnp.float32)[:, None] * new_row[None, :]

    return lax.fori_loop(0, order, row_step, jnp.zeros((order, order), jnp.float32))


def local(members, background):
    fields, rows, cols, width = members.shape
    nlat = rows * lax.axis_size("lat")
    first = lax.axis_index("lat") * rows
    kx_rows, unused_weight = row_coefs(first + jnp.arange(rows), nlat)
    padded = extended(members, (("lat", 1),), 1, False)
    padded = extended(padded, (("lon", 2),), 1, True)
    inner = smooth_pass(padded.astype(jnp.float32), kx_rows)
    padded = extended(inner, (("lat", 1),), 1, False)
    padded = extended(padded, (("lon", 2),), 1, True)
    final = smooth_pass(padded, kx_rows)
    unused_kx, weight = row_coefs(first + jnp.arange(rows), nlat)
    anomaly = (
        (final - background.astype(jnp.float32)[:, :, :, None]) * weight[None, :, None, None]
    ).astype(jnp.bfloat16)
    matrix = anomaly.reshape(-1, width)
    partial_gram = lax.dot_general(
        matrix, matrix, (((0,), (0,)), ((), ())), preferred_element_type=jnp.float32
    )
    gram = lax.psum(partial_gram, "lat")
    gram = lax.psum(gram, "lon")
    total_rows = fields * nlat * cols * lax.axis_size("lon")
    gram = gram / total_rows
    r_factor = chol_upper(gram)
    inverse = upper_inverse(r_factor)
    modes = jnp.dot(
        matrix, inverse, precision=lax.Precision.HIGHEST, preferred_element_type=jnp.float32
    )
    return (modes.reshape(fields, rows, cols, width), r_factor)


def solution(mesh):
    return jax.shard_map(
        local,
        mesh=mesh,
        in_specs=(P(None, "lat", "lon", None), P(None, "lat", "lon")),
        out_specs=(P(None, "lat", "lon", None), P()),
        check_vma=False,
    )
```

profile of v0, /device:TPU:0, one launch (start us, length us, event | category | flops | bytes accessed | tf_op | source)
XLA Modules:
  0.0 709.5 jit_solution(13157840494007377491)
XLA Ops:
  7.2 2.0 fusion.45
  9.3 3.5 collective-permute-start
  12.8 1.3 collective-permute-start.1
  14.1 1.6 collective-permute-done
  15.7 4.3 constant_dynamic-update-slice_fusion.1
  20.2 5.3 collective-permute-start.3
  25.6 1.8 collective-permute-done.2
  27.4 2.0 maximum_convert_fusion
  29.3 5.8 fusion.34
  35.2 4.4 collective-permute-start.4
  39.6 1.3 collective-permute-start.5
  40.9 4.9 collective-permute-done.4
  45.8 4.7 collective-permute-done.5
  50.7 4.3 collective-permute-start.6
  55.0 1.7 collective-permute-done.6
  56.7 5.4 collective-permute-done.7
  62.1 14.0 %fusion.27 = bf16[3,32,180,128]{3,2,1,0:T(8,128)(2,1)S(1)} fusion(f32[3,32,180,128]{3,2,1,0:T(8,128)S(1)} %fusion.34, f32[3,1,180,128]{3,2,1,0:T(8,128)S(1)} %collective-permute-done.4, f32[3,1,180,128]{3,2,1,0:T(8,128)S(1)} %collective-permute-done.5, f32[3,34,1,128]{3,2,1,0:T(1,128)S(1)} %collective-permute-done.7, ...), kind=kLoop, calls=%fused_computation.37 | loop fusion | flops 44236800 | bytes 13997824 | tf_op jit(solution)/shard_map/convert_element_type | solution.py:82
  76.2 2.1 copy-done
  78.2 2.0 convolution_bitcast_fusion.2
  80.5 73.0 %all-reduce.3.cloned.1.call-done = f32[128,128]{1,0:T(8,128)} async-done(((f32[128,128]{1,0:T(8,128)}), f32[128,128]{1,0:T(8,128)}) %all-reduce.3.cloned.1.call-update) | async-done | bytes 65552 | tf_op jit(solution)/shard_map/psum | solution.py:87
  153.6 129.1 %all-reduce.5.cloned.1.call-done = f32[128,128]{1,0:T(8,128)} async-done(((f32[128,128]{1,0:T(8,128)}), f32[128,128]{1,0:T(8,128)}) %all-reduce.5.cloned.1.call-update) | async-done | bytes 65552 | tf_op jit(solution)/shard_map/psum | solution.py:88
  282.7 0.8 broadcast_multiply_fusion
  283.6 213.3 %while.32 = (s32[]{:T(128)}, f32[128,128]{1,0:T(8,128)S(1)}, f32[128,128]{0,1:T(8,128)S(1)}, s32[]{:T(128)}, s32[]{:T(128)}) while((s32[]{:T(128)}, f32[128,128]{1,0:T(8,128)S(1)}, f32[128,128]{0,1:T(8,128)S(1)}, s32[]{:T(128)}, s32[]{:T(128)}) %tuple.88), condition=%wide.region_4.5_spmd.clone.clone, body=%wide.region_2.4_spmd.clone.clone.sunk | while | flops 263298 | bytes 333408 | solution.py:47
  283.7 0.8 fusion.56
  285.3 0.8 fusion.56
  290.3 0.8 fusion.56
  292.0 0.8 fusion.56
  293.7 0.8 fusion.56
  298.7 0.8 fusion.56
  300.3 0.8 fusion.56
  305.3 0.8 fusion.56
  307.0 0.8 fusion.56
  308.7 0.8 fusion.56
  313.7 0.8 fusion.56
  315.3 0.8 fusion.56
  317.0 0.8 fusion.56
  322.0 0.8 fusion.56
  323.7 0.8 fusion.56
  325.3 0.8 fusion.56
  330.3 0.8 fusion.56
  332.0 0.8 fusion.56
  337.0 0.8 fusion.56
  338.7 0.8 fusion.56
  340.3 0.8 fusion.56
  345.3 0.8 fusion.56
  347.0 0.8 fusion.56
  497.0 197.9 %while.33 = (s32[]{:T(128)}, f32[128,128]{1,0:T(8,128)S(1)}, f32[128,128]{1,0:T(8,128)S(1)}, f32[128,128]{1,0:T(8,128)S(1)}, s32[]{:T(128)}, /*index=5*/s32[]{:T(128)}, s32[]{:T(128)}, s32[]{:T(128)}) while((s32[]{:T(128)}, f32[128,128]{1,0:T(8,128)S(1)}, f32[128,128]{1,0:T(8,128)S(1)}, f32[128,128]{1,0:T(8,128)S(1)}, ...), condition=%wide.region_7.8_spmd.clone.clone, body=%wide.region_5.7_spmd.clone.clone.sunk | while | flops 263302 | bytes 202401 | solution.py:65
  694.9 7.7 %fusion.38 = f32[3,32,180,128]{3,1,2,0:T(8,128)} fusion(bf16[3,32,180,128]{3,2,1,0:T(8,128)(2,1)} %copy-done, f32[128,128]{1,0:T(8,128)S(1)} %get-tuple-element.220), kind=kOutput, calls=%fused_computation.58 | convolution fusion | flops 3397386240 | bytes 13336576 | tf_op jit(solution)/shard_map/dot_general | solution.py:93
  (1157 shorter events, 293.8 us)
Async XLA Ops:
  7.2 146.4 %all-reduce.3.cloned.1.call-start = ((), (), s32[]{:S(2)}) async-start(), calls=%async_computation | async-start | bytes 131072 | tf_op jit(solution)/shard_map/psum | solution.py:87
  9.3 6.4 collective-permute-start
  12.8 7.2 %collective-permute-start.1 = (bf16[3,1,180,128]{3,2,1,0:T(8,128)(2,1)S(1)}, bf16[3,1,180,128]{3,2,1,0:T(8,128)(2,1)S(1)}, u32[]{:S(2)}, u32[]{:S(2)}) collective-permute-start(bf16[3,1,180,128]{3,2,1,0:T(8,128)(2,1)S(1)} %copy.25), channel_id=1, source_target_pairs={{1,0},{2,1},{3,2},{4,3},{5,4},{6,5},{7,6},{9,8},{10,9},{11,10},{12... | collective-permute-start | bytes 414728 | tf_op jit(solution)/shard_map/ppermute | solution.py:16
  20.1 7.2 %collective-permute-start.2 = (bf16[3,34,1,128]{3,2,1,0:T(2,128)(2,1)S(1)}, bf16[3,34,1,128]{3,2,1,0:T(2,128)(2,1)S(1)}, u32[]{:S(2)}, u32[]{:S(2)}) collective-permute-start(bf16[3,34,1,128]{3,2,1,0:T(2,128)(2,1)S(1)} %get-tuple-element.308), channel_id=1, source_target_pairs={{0,8},{8,16},{16,24},{24,32},{32,40},{40,48},{48,56},{56,64},{64,7... | collective-permute-start | bytes 78344 | tf_op jit(solution)/shard_map/ppermute | solution.py:15
  20.2 7.2 %collective-permute-start.3 = (bf16[3,34,1,128]{3,2,1,0:T(2,128)(2,1)S(1)}, bf16[3,34,1,128]{3,2,1,0:T(2,128)(2,1)S(1)}, u32[]{:S(2)}, u32[]{:S(2)}) collective-permute-start(bf16[3,34,1,128]{3,2,1,0:T(2,128)(2,1)S(1)} %get-tuple-element.309), channel_id=1, source_target_pairs={{8,0},{16,8},{24,16},{32,24},{40,32},{48,40},{56,48},{64,56},{72,6... | collective-permute-start | bytes 78344 | tf_op jit(solution)/shard_map/ppermute | solution.py:16
  35.2 19.9 %copy-start.2 = (bf16[3,32,180]{2,1,0:T(8,128)(2,1)S(1)}, bf16[3,32,180]{2,1,0:T(8,128)(2,1)}, u32[]{:S(2)}) copy-start(bf16[3,32,180]{2,1,0:T(8,128)(2,1)} %param.7) | copy-start | bytes 103684
  35.2 10.6 %collective-permute-start.4 = (f32[3,1,180,128]{3,2,1,0:T(8,128)S(1)}, f32[3,1,180,128]{3,2,1,0:T(8,128)S(1)}, u32[]{:S(2)}, u32[]{:S(2)}) collective-permute-start(f32[3,1,180,128]{3,2,1,0:T(8,128)S(1)} %get-tuple-element.307), channel_id=1, source_target_pairs={{0,1},{1,2},{2,3},{3,4},{4,5},{5,6},{6,7},{8,9},{9,10},{10,11},{11... | collective-permute-start | bytes 829448 | tf_op jit(solution)/shard_map/ppermute | solution.py:15
  39.6 10.9 %collective-permute-start.5 = (f32[3,1,180,128]{3,2,1,0:T(8,128)S(1)}, f32[3,1,180,128]{3,2,1,0:T(8,128)S(1)}, u32[]{:S(2)}, u32[]{:S(2)}) collective-permute-start(f32[3,1,180,128]{3,2,1,0:T(8,128)S(1)} %get-tuple-element.306), channel_id=1, source_target_pairs={{1,0},{2,1},{3,2},{4,3},{5,4},{6,5},{7,6},{9,8},{10,9},{11,10},{12... | collective-permute-start | bytes 829448 | tf_op jit(solution)/shard_map/ppermute | solution.py:16
  50.7 6.1 collective-permute-start.6
  55.0 7.2 %collective-permute-start.7 = (f32[3,34,1,128]{3,2,1,0:T(1,128)S(1)}, f32[3,34,1,128]{3,2,1,0:T(1,128)S(1)}, u32[]{:S(2)}, u32[]{:S(2)}) collective-permute-start(f32[3,34,1,128]{3,2,1,0:T(1,128)S(1)} %get-tuple-element.305), channel_id=1, source_target_pairs={{0,8},{8,16},{16,24},{24,32},{32,40},{40,48},{48,56},{56,64},{64,7... | collective-permute-start | bytes 156680 | tf_op jit(solution)/shard_map/ppermute | solution.py:15
  76.2 2.1 copy-start
  80.3 202.4 %all-reduce.5.cloned.1.call-start = ((), (), s32[]{:S(2)}) async-start(), calls=%async_computation.1 | async-start | bytes 131072 | tf_op jit(solution)/shard_map/psum | solution.py:88
  694.9 7.8 %copy-start.1 = (f32[128,128]{1,0:T(8,128)}, f32[128,128]{1,0:T(8,128)S(1)}, u32[]{:S(2)}) copy-start(f32[128,128]{1,0:T(8,128)S(1)} %get-tuple-element.411) | copy-start | bytes 196612
Sparse Core Ops, SparseCore 0:
  80.4 73.1 all-reduce.2
  156.2 126.4 all-reduce.4
where the time goes:
time: 712 us; the launch traced here: 709 us
  waiting for transfers between devices  222 us (31%)
  matrix products  217 us (30%)
  other arithmetic  127 us (18%)
  loops' own time  99.4 us (14%)
  starting transfers between devices  20.5 us (3%)
  between operations  14.3 us (2%)
  local copies, waits for them, and re-layouts  8.73 us (1%)
    psum x1, waiting for transfers between devices, local(): gram = lax.psum(gram, 'lon')  129 us
    dot_general x128, matrix products, column(): resid = col_g - jnp.dot(lower, row_j, precision=lax.Precision.HIGHEST)  105 us
    dot_general x128, matrix products, row_step(): jnp.dot(above, solved, precision=lax.Precision.HIGHEST)  102 us
    another operation x1, loops' own time, chol_upper(): lax.fori_loop(0, order, column, jnp.zeros((order, order), jnp.float32))  94.9 us
    reduce_sum x128, other arithmetic, row_step(): diag = jnp.sum(jnp.where(index == i, row_u, 0.0))  77.7 us
    psum x1, waiting for transfers between devices, local(): gram = lax.psum(partial_gram, 'lat')  73 us
  transfers between devices with their start and end apart: 10, of which 8 were waited for; matrix products, arithmetic and copies ran while one was open for 1% of the time, Pallas kernels for 0%

commit v1 on v0

--- a/solution.py
+++ b/solution.py
@@ -84,7 +84,7 @@
     partial_gram = lax.dot_general(
         matrix, matrix, (((0,), (0,)), ((), ())), preferred_element_type=jnp.float32
     )
-    gram = lax.psum(partial_gram, "lat")
+    gram = jnp.sum(lax.all_gather(partial_gram, "lat"), axis=0)
     gram = lax.psum(gram, "lon")
     total_rows = fields * nlat * cols * lax.axis_size("lon")
     gram = gram / total_rows

time: 712 us -> 674 us (0.947)
  waiting for transfers between devices: 222 us -> 148 us
  blocking collectives: 0 us -> 29.3 us
  other arithmetic: 127 us -> 135 us
    psum x1 -> x0, waiting for transfers between devices: 73 us -> none  [local(): gram = lax.psum(partial_gram, 'lat')]
    all_gather x0 -> x1, blocking collectives: none -> 29.3 us  [local(): gram = jnp.sum(lax.all_gather(partial_gram, 'lat'), axis=0)]
    convert_element_type x1, other arithmetic: 14 us -> 21.4 us  [local(): anomaly = ((final - background.astype(jnp.float32)[:, :, :, None]) * weig...]
  transfers between devices with their start and end apart: 10 -> 9, of which waited for: 8 -> 7; matrix products, arithmetic and copies ran while one was open for 1% -> 1% of each run, Pallas kernels for 0% -> 0%
where the time goes in v1:
time: 674 us; the launch traced here: 671 us
  matrix products  217 us (32%)
  waiting for transfers between devices  148 us (22%)
  other arithmetic  135 us (20%)
  loops' own time  99.4 us (15%)
  blocking collectives  29.3 us (4%)
  starting transfers between devices  20.4 us (3%)
  between operations  14.3 us (2%)
  local copies, waits for them, and re-layouts  8.73 us (1%)
    psum x1, waiting for transfers between devices, local(): gram = lax.psum(gram, 'lon')  128 us
    dot_general x128, matrix products, column(): resid = col_g - jnp.dot(lower, row_j, precision=lax.Precision.HIGHEST)  105 us
    dot_general x128, matrix products, row_step(): jnp.dot(above, solved, precision=lax.Precision.HIGHEST)  102 us
    another operation x1, loops' own time, chol_upper(): lax.fori_loop(0, order, column, jnp.zeros((order, order), jnp.float32))  94.9 us
    reduce_sum x128, other arithmetic, row_step(): diag = jnp.sum(jnp.where(index == i, row_u, 0.0))  77.7 us
    all_gather x1, blocking collectives, local(): gram = jnp.sum(lax.all_gather(partial_gram, 'lat'), axis=0)  29.3 us
    convert_element_type x1, other arithmetic, local(): anomaly = ((final - background.astype(jnp.float32)[:, :, :, None]) * weig...  21.4 us
    ppermute x4, waiting for transfers between devices, extended(): before = lax.ppermute(last, axis, up)  13.7 us
  transfers between devices with their start and end apart: 9, of which 7 were waited for; matrix products, arithmetic and copies ran while one was open for 1% of the time, Pallas kernels for 0%

profile of v1, /device:TPU:0, one launch (start us, length us, event | category | flops | bytes accessed | tf_op | source)
XLA Modules:
  0.0 671.5 jit_solution(3673813644483842590)
XLA Ops:
  7.2 2.0 fusion.45
  9.3 3.5 collective-permute-start
  12.8 1.3 collective-permute-start.1
  14.1 1.6 collective-permute-done
  15.7 4.3 constant_dynamic-update-slice_fusion.1
  20.2 5.3 collective-permute-start.3
  25.6 1.8 collective-permute-done.2
  27.4 2.0 maximum_convert_fusion
  29.3 5.8 fusion.34
  35.2 4.5 collective-permute-start.4
  39.8 1.3 collective-permute-start.5
  41.1 4.9 collective-permute-done.4
  46.0 4.7 collective-permute-done.5
  50.8 4.3 collective-permute-start.6
  55.2 1.7 collective-permute-done.6
  56.9 5.4 collective-permute-done.7
  62.3 21.4 %fusion.27 = bf16[3,32,180,128]{3,2,1,0:T(8,128)(2,1)S(1)} fusion(f32[3,32,180,128]{3,2,1,0:T(8,128)} %copy-done, f32[3,1,180,128]{3,2,1,0:T(8,128)S(1)} %collective-permute-done.4, f32[3,1,180,128]{3,2,1,0:T(8,128)S(1)} %collective-permute-done.5, f32[3,34,1,128]{3,2,1,0:T(1,128)S(1)} %collective-permute-done.7, ...), kind=kLoop, calls=%fused_computation.37 | loop fusion | flops 44236800 | bytes 13997824 | tf_op jit(solution)/shard_map/convert_element_type | solution.py:82
  83.7 2.0 copy-done.1
  85.8 1.4 convolution_bitcast_fusion.2
  87.2 29.3 %all-gather = f32[1024,128]{1,0:T(8,128)S(1)} all-gather(f32[128,128]{1,0:T(8,128)S(1)} %convolution_bitcast_fusion.2), channel_id=2, replica_groups=mesh['lon'=16,'lat'=8] {'lat'}, dimensions={0}, use_global_device_ids=true | all-gather | bytes 589824 | tf_op jit(solution)/shard_map/all_gather | solution.py:87
  117.1 127.5 %all-reduce.2.cloned.1.call-done = f32[128,128]{1,0:T(8,128)} async-done(((f32[128,128]{1,0:T(8,128)}), f32[128,128]{1,0:T(8,128)}) %all-reduce.2.cloned.1.call-update) | async-done | bytes 65552 | tf_op jit(solution)/shard_map/psum | solution.py:88
  244.7 0.8 broadcast_multiply_fusion
  245.6 213.3 %while.32 = (s32[]{:T(128)}, f32[128,128]{1,0:T(8,128)S(1)}, f32[128,128]{0,1:T(8,128)S(1)}, s32[]{:T(128)}, s32[]{:T(128)}) while((s32[]{:T(128)}, f32[128,128]{1,0:T(8,128)S(1)}, f32[128,128]{0,1:T(8,128)S(1)}, s32[]{:T(128)}, s32[]{:T(128)}) %tuple.87), condition=%wide.region_4.5_spmd.clone.clone, body=%wide.region_2.4_spmd.clone.clone.sunk | while | flops 263298 | bytes 333408 | solution.py:47
  245.7 0.8 fusion.56
  247.3 0.8 fusion.56
  252.3 0.8 fusion.56
  254.0 0.8 fusion.56
  255.6 0.8 fusion.56
  260.6 0.8 fusion.56
  262.3 0.8 fusion.56
  264.0 0.8 fusion.56
  269.0 0.8 fusion.56
  270.6 0.8 fusion.56
  272.3 0.8 fusion.56
  277.3 0.8 fusion.56
  279.0 0.8 fusion.56
  284.0 0.8 fusion.56
  285.6 0.8 fusion.56
  287.3 0.8 fusion.56
  292.3 0.8 fusion.56
  294.0 0.8 fusion.56
  295.6 0.8 fusion.56
  300.6 0.8 fusion.56
  302.3 0.8 fusion.56
  304.0 0.8 fusion.56
  309.0 0.8 fusion.56
  459.0 197.9 %while.33 = (s32[]{:T(128)}, f32[128,128]{1,0:T(8,128)S(1)}, f32[128,128]{1,0:T(8,128)S(1)}, f32[128,128]{1,0:T(8,128)S(1)}, s32[]{:T(128)}, /*index=5*/s32[]{:T(128)}, s32[]{:T(128)}, s32[]{:T(128)}) while((s32[]{:T(128)}, f32[128,128]{1,0:T(8,128)S(1)}, f32[128,128]{1,0:T(8,128)S(1)}, f32[128,128]{1,0:T(8,128)S(1)}, ...), condition=%wide.region_7.8_spmd.clone.clone, body=%wide.region_5.7_spmd.clone.clone.sunk | while | flops 263302 | bytes 202401 | solution.py:65
  656.9 7.7 %fusion.38 = f32[3,32,180,128]{3,1,2,0:T(8,128)} fusion(bf16[3,32,180,128]{3,2,1,0:T(8,128)(2,1)} %copy-done.1, f32[128,128]{1,0:T(8,128)S(1)} %get-tuple-element.220), kind=kOutput, calls=%fused_computation.58 | convolution fusion | flops 3397386240 | bytes 13336576 | tf_op jit(solution)/shard_map/dot_general | solution.py:93
  (1158 shorter events, 294.2 us)
Async XLA Ops:
  7.2 237.5 %all-reduce.2.cloned.1.call-start = ((), (), s32[]{:S(2)}) async-start(), calls=%async_computation | async-start | bytes 131072 | tf_op jit(solution)/shard_map/psum | solution.py:88
  9.3 6.4 collective-permute-start
  12.8 7.2 %collective-permute-start.1 = (bf16[3,1,180,128]{3,2,1,0:T(8,128)(2,1)S(1)}, bf16[3,1,180,128]{3,2,1,0:T(8,128)(2,1)S(1)}, u32[]{:S(2)}, u32[]{:S(2)}) collective-permute-start(bf16[3,1,180,128]{3,2,1,0:T(8,128)(2,1)S(1)} %copy.24), channel_id=1, source_target_pairs={{1,0},{2,1},{3,2},{4,3},{5,4},{6,5},{7,6},{9,8},{10,9},{11,10},{12... | collective-permute-start | bytes 414728 | tf_op jit(solution)/shard_map/ppermute | solution.py:16
  20.1 7.2 %collective-permute-start.2 = (bf16[3,34,1,128]{3,2,1,0:T(2,128)(2,1)S(1)}, bf16[3,34,1,128]{3,2,1,0:T(2,128)(2,1)S(1)}, u32[]{:S(2)}, u32[]{:S(2)}) collective-permute-start(bf16[3,34,1,128]{3,2,1,0:T(2,128)(2,1)S(1)} %get-tuple-element.305), channel_id=1, source_target_pairs={{0,8},{8,16},{16,24},{24,32},{32,40},{40,48},{48,56},{56,64},{64,7... | collective-permute-start | bytes 78344 | tf_op jit(solution)/shard_map/ppermute | solution.py:15
  20.2 7.2 %collective-permute-start.3 = (bf16[3,34,1,128]{3,2,1,0:T(2,128)(2,1)S(1)}, bf16[3,34,1,128]{3,2,1,0:T(2,128)(2,1)S(1)}, u32[]{:S(2)}, u32[]{:S(2)}) collective-permute-start(bf16[3,34,1,128]{3,2,1,0:T(2,128)(2,1)S(1)} %get-tuple-element.306), channel_id=1, source_target_pairs={{8,0},{16,8},{24,16},{32,24},{40,32},{48,40},{56,48},{64,56},{72,6... | collective-permute-start | bytes 78344 | tf_op jit(solution)/shard_map/ppermute | solution.py:16
  35.2 15.6 %copy-start = (f32[3,32,180,128]{3,2,1,0:T(8,128)}, f32[3,32,180,128]{3,2,1,0:T(8,128)S(1)}, u32[]{:S(2)}) copy-start(f32[3,32,180,128]{3,2,1,0:T(8,128)S(1)} %fusion.34) | copy-start | bytes 26542084
  35.2 20.0 %copy-start.3 = (bf16[3,32,180]{2,1,0:T(8,128)(2,1)S(1)}, bf16[3,32,180]{2,1,0:T(8,128)(2,1)}, u32[]{:S(2)}) copy-start(bf16[3,32,180]{2,1,0:T(8,128)(2,1)} %param.7) | copy-start | bytes 103684
  35.2 10.8 %collective-permute-start.4 = (f32[3,1,180,128]{3,2,1,0:T(8,128)S(1)}, f32[3,1,180,128]{3,2,1,0:T(8,128)S(1)}, u32[]{:S(2)}, u32[]{:S(2)}) collective-permute-start(f32[3,1,180,128]{3,2,1,0:T(8,128)S(1)} %get-tuple-element.304), channel_id=1, source_target_pairs={{0,1},{1,2},{2,3},{3,4},{4,5},{5,6},{6,7},{8,9},{9,10},{10,11},{11... | collective-permute-start | bytes 829448 | tf_op jit(solution)/shard_map/ppermute | solution.py:15
  39.8 10.9 %collective-permute-start.5 = (f32[3,1,180,128]{3,2,1,0:T(8,128)S(1)}, f32[3,1,180,128]{3,2,1,0:T(8,128)S(1)}, u32[]{:S(2)}, u32[]{:S(2)}) collective-permute-start(f32[3,1,180,128]{3,2,1,0:T(8,128)S(1)} %get-tuple-element.303), channel_id=1, source_target_pairs={{1,0},{2,1},{3,2},{4,3},{5,4},{6,5},{7,6},{9,8},{10,9},{11,10},{12... | collective-permute-start | bytes 829448 | tf_op jit(solution)/shard_map/ppermute | solution.py:16
  50.8 6.1 collective-permute-start.6
  55.1 7.2 %collective-permute-start.7 = (f32[3,34,1,128]{3,2,1,0:T(1,128)S(1)}, f32[3,34,1,128]{3,2,1,0:T(1,128)S(1)}, u32[]{:S(2)}, u32[]{:S(2)}) collective-permute-start(f32[3,34,1,128]{3,2,1,0:T(1,128)S(1)} %get-tuple-element.302), channel_id=1, source_target_pairs={{0,8},{8,16},{16,24},{24,32},{32,40},{40,48},{48,56},{56,64},{64,7... | collective-permute-start | bytes 156680 | tf_op jit(solution)/shard_map/ppermute | solution.py:15
  83.7 2.1 copy-start.1
  656.9 7.8 %copy-start.2 = (f32[128,128]{1,0:T(8,128)}, f32[128,128]{1,0:T(8,128)S(1)}, u32[]{:S(2)}) copy-start(f32[128,128]{1,0:T(8,128)S(1)} %get-tuple-element.407) | copy-start | bytes 196612
Sparse Core Ops, SparseCore 0:
  117.2 127.3 all-reduce.1
